TPU v7x, 32 devices: a whole 2x2x4 slice. The times are simulated.
32 devices in a mesh: prow: 8 (over z, y), pcol: 4 (over x, core).
Axes of the slice: x: 2, y: 2, z: 4, core: 2. Of those that a mesh axis runs over, the one named last changes fastest.
Arguments:
- inverse_tiles: bfloat16 [24576, 24576], P('prow', 'pcol'), may hold values from -6 to 6
- panel_blocks: bfloat16 [24576, 1536], P(('prow', 'pcol')), may hold values from -0.0546875 to 0.0546875
- pivot_inverse: bfloat16 [3, 512, 512], replicated, may hold values from -0.25 to 0.25
- diagonal_inverse: float32 [3, 512, 512], replicated, may hold values from -6 to 6
- ancestors: int32 [3, 24], replicated, may hold values from 0 to 47, all different within a row
Outputs:
- cross_blocks: float32 [24576, 1536], P(('prow', 'pcol'))
- diagonal_blocks: float32 [3, 512, 512], replicated
Inputs may be any that keep to these rules, and one draw needn't show every extreme that they name: `ancestors`: each row names 24 different blocks, and every block is named by some row.
All inputs are finite; a program needn't handle non-finite values.
Results may differ from a plain program's by a relative error of at most 0.003.
Values may be sent and summed in bfloat16 or wider, within the bound.
A program may use at most 128 MiB of HBM per device.

v0:
```python
import jax
import jax.numpy as jnp
from jax import lax
from jax.sharding import PartitionSpec as P


def spread(value, axis, source):
    kept = jnp.where(lax.axis_index(axis) == source, value, 0).astype(value.dtype)
    return lax.psum(kept, axis)


def row_terms(inverse_tiles, columns):
    return jnp.dot(inverse_tiles, columns, preferred_element_type=jnp.float32)


def on_device(inverse_tiles, panel_blocks, pivot_inverse, diagonal_inverse, ancestors):
    seg_rows = panel_blocks.shape[0]
    n_super = pivot_inverse.shape[0]
    width = pivot_inverse.shape[1]
    row_devices = lax.axis_size("prow")
    col_devices = lax.axis_size("pcol")
    segment = lax.axis_index("prow") * col_devices + lax.axis_index("pcol")
    row_ids = segment * seg_rows + lax.iota(jnp.int32, seg_rows)
    block_ids = row_ids // width
    listed = jnp.any(block_ids[:, None, None] == ancestors[None, :, :], axis=2).astype(jnp.float32)
    raw_three = panel_blocks.reshape(seg_rows, n_super, width)
    normed = jnp.einsum(
        "rsw,swv->rsv", raw_three, pivot_inverse, preferred_element_type=jnp.float32
    )
    scaled = (normed * listed[:, :, None]).astype(jnp.bfloat16)
    own_panel = scaled.reshape(seg_rows, n_super * width)
    row_panel = lax.all_gather(own_panel, "pcol", axis=0, tiled=True)
    ratio = row_devices // col_devices
    pieces = []
    for offset in range(ratio):
        pieces.append(spread(row_panel, "prow", lax.axis_index("pcol") * ratio + offset))
    column_panel = jnp.concatenate(pieces, axis=0)
    summed = lax.psum_scatter(
        row_terms(inverse_tiles, column_panel), "pcol", scatter_dimension=0, tiled=True
    )
    cross = -(summed.reshape(seg_rows, n_super, width) * listed[:, :, None])
    local_terms = jnp.einsum(
        "rsw,rsv->swv", scaled.astype(jnp.float32), cross, precision=lax.Precision.HIGHEST
    )
    total = lax.psum(local_terms, ("prow", "pcol"))
    diagonal = diagonal_inverse - total
    return (cross.reshape(seg_rows, n_super * width), diagonal)


def solution(mesh):
    in_specs = (P("prow", "pcol"), P(("prow", "pcol"), None), P(), P(), P())
    out_specs = (P(("prow", "pcol"), None), P())
    return jax.shard_map(
        on_device, mesh=mesh, in_specs=in_specs, out_specs=out_specs, check_vma=False
    )
```

profile of v0, /device:TPU:0, one launch (start us, length us, event | category | flops | bytes accessed | tf_op | source)
XLA Modules:
  0.0 1028.7 jit_solution(8723417123079161685)
XLA Ops:
  7.2 0.0 copy-start
  7.2 0.0 all-gather.2.cloned.1.call-start
  7.3 0.9 compare_reduce_fusion
  8.2 0.0 copy-start.2
  8.2 4.3 copy.16
  12.4 0.0 copy-done
  12.4 4.5 fusion.8
  17.0 0.0 copy-done.2
  17.0 0.0 all-gather.2.cloned.1.call-update
  17.0 0.0 all-reduce.6.cloned.1.call-start
  17.0 67.0 %all-gather.2.cloned.1.call-done = bf16[3072,1536]{0,1:T(8,128)(2,1)} async-done(((bf16[768,1536]{0,1:T(8,128)(2,1)}), bf16[3072,1536]{0,1:T(8,128)(2,1)}) %all-gather.2.cloned.1.call-update) | async-done | bytes 9437200 | tf_op jit(solution)/shard_map/all_gather | solution.py:32
  84.1 10.7 %broadcast_select_fusion.1 = (bf16[3072,1536]{0,1:T(8,128)(2,1)}, bf16[3072,1536]{0,1:T(8,128)(2,1)}) fusion(bf16[3072,1536]{0,1:T(8,128)(2,1)} %all-gather.2.cloned.1.call-done, pred[]{:T(512)S(6)} %eq.19, pred[]{:T(512)S(6)} %eq.23), kind=kLoop, calls=%fused_computation.6 | loop fusion | flops 9437184 | bytes 28311554 | tf_op jit(solution)/shard_map/jit(_where)/select_n | solution.py:8
  94.8 0.0 all-reduce.6.cloned.1.call-update
  94.8 0.0 reduce-scatter.2.cloned.1.call-start
  94.9 567.5 %all-reduce.6.cloned.1.call-done = (bf16[3072,1536]{0,1:T(8,128)(2,1)}, bf16[3072,1536]{0,1:T(8,128)(2,1)}) async-done(((bf16[3072,1536]{0,1:T(8,128)(2,1)}, bf16[3072,1536]{0,1:T(8,128)(2,1)}), (bf16[3072,1536]{0,1:T(8,128)(2,1)}, bf16[3072,1536]{0,1:T(8,128)(2,1)})) %all-reduce.6.cloned.1.call-update) | async-done | bytes 18874384 | tf_op jit(solution)/shard_map/psum | solution.py:9
  662.4 70.5 %fusion.4 = f32[3072,1536]{0,1:T(8,128)} fusion(bf16[3072,6144]{1,0:T(8,128)(2,1)} %param.5, bf16[3072,1536]{0,1:T(8,128)(2,1)} %get-tuple-element.8, bf16[3072,1536]{0,1:T(8,128)(2,1)} %get-tuple-element.9), kind=kOutput, calls=%fused_computation.4 | convolution fusion | flops 58019807232 | bytes 75497472 | tf_op jit(solution)/shard_map/dot_general | solution.py:13
  732.9 0.0 copy-start.3
  732.9 0.0 reduce-scatter.2.cloned.1.call-update
  732.9 0.2 all-reduce.4.cloned.1.call-start
  733.2 136.7 %reduce-scatter.2.cloned.1.call-done = f32[768,1536]{0,1:T(8,128)} async-done(((f32[3072,1536]{0,1:T(8,128)}), f32[768,1536]{0,1:T(8,128)}) %reduce-scatter.2.cloned.1.call-update) | async-done | bytes 4718608 | tf_op jit(solution)/shard_map/reduce_scatter | solution.py:38
  869.8 0.0 copy-done.3
  869.8 8.8 fusion.9
  878.6 0.0 all-reduce.4.cloned.1.call-update
  878.6 4.8 fusion.7
  883.4 0.0 copy-start.1
  883.4 6.4 copy.20
  889.9 127.0 %all-reduce.4.cloned.1.call-done = f32[3,512,512]{2,1,0:T(8,128)} async-done(((f32[3,512,512]{2,1,0:T(8,128)}), f32[3,512,512]{2,1,0:T(8,128)}) %all-reduce.4.cloned.1.call-update) | async-done | bytes 3145744 | tf_op jit(solution)/shard_map/psum | solution.py:45
  1016.9 5.3 sub.10
  1022.2 0.0 copy-done.1
  (2 shorter events, 0.0 us)
Async XLA Ops:
  7.2 5.3 copy-start
  7.2 76.9 %all-gather.2.cloned.1.call-start = ((), (), s32[]{:S(2)}) async-start(), calls=%async_computation.1 | async-start | bytes 11796480 | tf_op jit(solution)/shard_map/all_gather | solution.py:32
  8.2 8.8 copy-start.2
  17.0 645.4 %all-reduce.6.cloned.1.call-start = ((), (), s32[]{:S(2)}) async-start(), calls=%async_computation.4 | async-start | bytes 37748736 | tf_op jit(solution)/shard_map/psum | solution.py:9
  94.8 775.0 %reduce-scatter.2.cloned.1.call-start = ((), (), s32[]{:S(2)}) async-start(), calls=%async_computation.2 | async-start | bytes 23592960 | tf_op jit(solution)/shard_map/reduce_scatter | solution.py:38
  732.9 136.9 %copy-start.3 = (f32[768,3]{0,1:T(4,128)S(1)}, f32[768,3]{0,1:T(4,128)}, u32[]{:S(2)}) copy-start(f32[768,3]{0,1:T(4,128)} %copy-done.2) | copy-start | bytes 27652
  732.9 284.0 %all-reduce.4.cloned.1.call-start = ((), (), s32[]{:S(2)}) async-start(), calls=%async_computation.3 | async-start | bytes 6291456 | tf_op jit(solution)/shard_map/psum | solution.py:45
  883.4 138.7 %copy-start.1 = (bf16[3,512,512]{2,1,0:T(8,128)(2,1)S(1)}, bf16[3,512,512]{2,1,0:T(8,128)(2,1)}, u32[]{:S(2)}) copy-start(bf16[3,512,512]{2,1,0:T(8,128)(2,1)} %param.7) | copy-start | bytes 4718596
Sparse Core Ops, SparseCore 0:
  17.1 66.9 all-gather.1
  94.9 567.4 all-reduce.5
  733.0 136.7 reduce-scatter.1
  878.8 138.0 all-reduce.3
where the time goes:
time: 1030 us
  waiting for transfers between devices  898 us (87%)
  matrix products  83.8 us (8%)
  other arithmetic  21.7 us (2%)
  between operations  13.8 us (1%)
  local copies, waits for them, and re-layouts  10.7 us (1%)
    psum x1, waiting for transfers between devices, spread(): return lax.psum(kept, axis)  568 us
    reduce_scatter x1, waiting for transfers between devices, on_device(): lax.psum_scatter(row_terms(inverse_tiles, column_panel), 'pcol', scatter_...  137 us
    psum x1, waiting for transfers between devices, on_device(): total = lax.psum(local_terms, ('prow', 'pcol'))  127 us
    dot_general x1, matrix products, row_terms(): return jnp.dot(inverse_tiles, columns, preferred_element_type=jnp.float32)  70.5 us
    all_gather x1, waiting for transfers between devices, on_device(): row_panel = lax.all_gather(own_panel, 'pcol', axis=0, tiled=True)  67 us
  transfers between devices with their start and end apart: 4, of which 4 were waited for; matrix products, arithmetic and copies ran while one was open for 1% of the time, Pallas kernels for 0%

commit v1 on v0

--- a/solution.py
+++ b/solution.py
@@ -29,7 +29,33 @@
     )
     scaled = (normed * listed[:, :, None]).astype(jnp.bfloat16)
     own_panel = scaled.reshape(seg_rows, n_super * width)
-    row_panel = lax.all_gather(own_panel, "pcol", axis=0, tiled=True)
+
+    def close_the_packet(view):
+        along_axis = "pcol"
+        axis_n = lax.axis_size(along_axis)
+        idx = 0
+        buffer = []
+        while idx < axis_n:
+            buffer.append((idx, (idx + 1) % axis_n))
+            idx = idx + 1
+        pieces_in = []
+        idx = 0
+        while idx < axis_n:
+            pieces_in.append((idx, (idx - 1) % axis_n))
+            idx = idx + 1
+        local_part, reply = ([view], [view])
+        for _ in range(axis_n // 2):
+            local_part.append(lax.ppermute(local_part[-1], axis_name=along_axis, perm=buffer))
+        tick = 0
+        while tick < (axis_n - 1) // 2:
+            reply.append(lax.ppermute(reply[-1], axis_name=along_axis, perm=pieces_in))
+            tick = tick + 1
+        f_next = jnp.concatenate([*local_part[::-1], *reply[1:]], 0)
+        return jnp.roll(
+            f_next, shift=(lax.axis_index(along_axis) - axis_n // 2) * view.shape[0], axis=0
+        )
+
+    row_panel = close_the_packet(own_panel)
     ratio = row_devices // col_devices
     pieces = []
     for offset in range(ratio):

time: 1030 us -> 1060 us (1.029)
  local copies, waits for them, and re-layouts: 10.7 us -> 26.5 us
  waiting for transfers between devices: 898 us -> 913 us
    ppermute x0 -> x3, waiting for transfers between devices: none -> 78.3 us  [the longest x2 78.3 us: close_the_packet(): lax.ppermute(local_part[-1], axis_name=along_axis, perm=buffer)]
    all_gather x1 -> x0, waiting for transfers between devices: 67 us -> none  [on_device(): row_panel = lax.all_gather(own_panel, 'pcol', axis=0, tiled=True)]
    unnamed x10 -> x17, local copies, waits for them, and re-layouts: 10.7 us -> 24.5 us
  transfers between devices with their start and end apart: 4 -> 6, of which waited for: 4 -> 5; matrix products, arithmetic and copies ran while one was open for 1% -> 2% of each run, Pallas kernels for 0% -> 0%
where the time goes in v1:
time: 1060 us
  waiting for transfers between devices  913 us (86%)
  matrix products  83.8 us (8%)
  local copies, waits for them, and re-layouts  26.5 us (2%)
  other arithmetic  20.8 us (2%)
  between operations  13.9 us (1%)
    psum x1, waiting for transfers between devices, spread(): return lax.psum(kept, axis)  571 us
    reduce_scatter x1, waiting for transfers between devices, on_device(): lax.psum_scatter(row_terms(inverse_tiles, column_panel), 'pcol', scatter_...  137 us
    psum x1, waiting for transfers between devices, on_device(): total = lax.psum(local_terms, ('prow', 'pcol'))  127 us
    ppermute x2, waiting for transfers between devices, close_the_packet(): lax.ppermute(local_part[-1], axis_name=along_axis, perm=buffer)  78.3 us
    dot_general x1, matrix products, row_terms(): return jnp.dot(inverse_tiles, columns, preferred_element_type=jnp.float32)  70.5 us
    unnamed x17, local copies, waits for them, and re-layouts  24.5 us
  transfers between devices with their start and end apart: 6, of which 5 were waited for; matrix products, arithmetic and copies ran while one was open for 2% of the time, Pallas kernels for 0%

profile of v1, /device:TPU:0, one launch (start us, length us, event | category | flops | bytes accessed | tf_op | source)
XLA Modules:
  0.0 1060.8 jit_solution(7966347351701540537)
XLA Ops:
  7.2 0.0 copy-start
  7.2 0.0 all-reduce.6.cloned.1.call-start
  7.2 0.9 compare_reduce_fusion
  8.2 0.0 copy-start.2
  8.2 4.3 copy.16
  12.4 0.0 copy-done
  12.4 4.5 fusion.8
  17.0 0.5 collective-permute-start
  17.4 28.8 %collective-permute-done = bf16[768,1536]{0,1:T(8,128)(2,1)} collective-permute-done((bf16[768,1536]{0,1:T(8,128)(2,1)}, bf16[768,1536]{0,1:T(8,128)(2,1)}, u32[]{:S(2)}, u32[]{:S(2)}) %collective-permute-start) | collective-permute-done | bytes 2359328 | tf_op jit(solution)/shard_map/ppermute | solution.py:48
  46.2 0.0 collective-permute-start.1
  46.2 1.7 collective-permute-start.2
  48.0 49.5 %collective-permute-done.1 = bf16[768,1536]{0,1:T(8,128)(2,1)} collective-permute-done((bf16[768,1536]{0,1:T(8,128)(2,1)}, bf16[768,1536]{0,1:T(8,128)(2,1)}, u32[]{:S(2)}, u32[]{:S(2)}) %collective-permute-start.1) | collective-permute-done | bytes 2359328 | tf_op jit(solution)/shard_map/ppermute | solution.py:48
  97.5 2.0 constant_dynamic-update-slice_fusion.7
  99.5 2.0 constant_dynamic-update-slice_fusion.6
  101.5 0.0 copy-done.2
  101.5 2.0 constant_dynamic-update-slice_fusion.5
  103.5 0.0 collective-permute-done.2
  103.5 2.0 constant_dynamic-update-slice_fusion.4
  105.5 2.0 constant_dynamic-update-slice_fusion.3
  107.5 2.0 constant_dynamic-update-slice_fusion.2
  109.5 2.0 constant_dynamic-update-slice_fusion.1
  111.5 2.0 constant_dynamic-update-slice_fusion
  113.5 9.7 broadcast_select_fusion.1
  123.2 0.0 all-reduce.6.cloned.1.call-update
  123.2 0.2 reduce-scatter.2.cloned.1.call-start
  123.4 571.1 %all-reduce.6.cloned.1.call-done = (bf16[3072,1536]{0,1:T(8,128)(2,1)}, bf16[3072,1536]{0,1:T(8,128)(2,1)}) async-done(((bf16[3072,1536]{0,1:T(8,128)(2,1)}, bf16[3072,1536]{0,1:T(8,128)(2,1)}), (bf16[3072,1536]{0,1:T(8,128)(2,1)}, bf16[3072,1536]{0,1:T(8,128)(2,1)})) %all-reduce.6.cloned.1.call-update) | async-done | bytes 18874384 | tf_op jit(solution)/shard_map/psum | solution.py:9
  694.5 70.5 %fusion.4 = f32[3072,1536]{0,1:T(8,128)} fusion(bf16[3072,6144]{1,0:T(8,128)(2,1)} %param.5, bf16[3072,1536]{0,1:T(8,128)(2,1)} %get-tuple-element.8, bf16[3072,1536]{0,1:T(8,128)(2,1)} %get-tuple-element.9), kind=kOutput, calls=%fused_computation.4 | convolution fusion | flops 58019807232 | bytes 75497472 | tf_op jit(solution)/shard_map/dot_general | solution.py:13
  765.0 0.0 copy-start.3
  765.0 0.0 reduce-scatter.2.cloned.1.call-update
  765.1 0.3 all-reduce.4.cloned.1.call-start
  765.3 136.6 %reduce-scatter.2.cloned.1.call-done = f32[768,1536]{0,1:T(8,128)} async-done(((f32[3072,1536]{0,1:T(8,128)}), f32[768,1536]{0,1:T(8,128)}) %reduce-scatter.2.cloned.1.call-update) | async-done | bytes 4718608 | tf_op jit(solution)/shard_map/reduce_scatter | solution.py:64
  902.0 0.0 copy-done.3
  902.0 8.8 fusion.9
  910.7 0.0 all-reduce.4.cloned.1.call-update
  910.8 0.0 copy-start.1
  910.8 4.9 fusion.7
  915.7 6.3 copy.20
  922.0 127.1 %all-reduce.4.cloned.1.call-done = f32[3,512,512]{2,1,0:T(8,128)} async-done(((f32[3,512,512]{2,1,0:T(8,128)}), f32[3,512,512]{2,1,0:T(8,128)}) %all-reduce.4.cloned.1.call-update) | async-done | bytes 3145744 | tf_op jit(solution)/shard_map/psum | solution.py:71
  1049.0 5.3 sub.19
  1054.3 0.0 copy-done.1
  (2 shorter events, 0.0 us)
Async XLA Ops:
  7.2 5.3 copy-start
  7.2 687.4 %all-reduce.6.cloned.1.call-start = ((), (), s32[]{:S(2)}) async-start(), calls=%async_computation.3 | async-start | bytes 37748736 | tf_op jit(solution)/shard_map/psum | solution.py:9
  8.2 93.3 %copy-start.2 = (f32[768,3]{0,1:T(4,128)}, f32[768,3]{0,1:T(4,128)S(1)}, u32[]{:S(2)}) copy-start(f32[768,3]{0,1:T(4,128)S(1)} %convert_element_type.14) | copy-start | bytes 27652
  17.0 29.2 %collective-permute-start = (bf16[768,1536]{0,1:T(8,128)(2,1)}, bf16[768,1536]{0,1:T(8,128)(2,1)}, u32[]{:S(2)}, u32[]{:S(2)}) collective-permute-start(bf16[768,1536]{0,1:T(8,128)(2,1)} %bitcast.2), channel_id=1, source_target_pairs={{0,1},{1,2},{2,3},{3,0},{4,5},{5,6},{6,7},{7,4},{8,9},{9,10},{10,1... | collective-permute-start | bytes 7077896 | tf_op jit(solution)/shard_map/ppermute | solution.py:48
  46.2 51.3 %collective-permute-start.1 = (bf16[768,1536]{0,1:T(8,128)(2,1)}, bf16[768,1536]{0,1:T(8,128)(2,1)}, u32[]{:S(2)}, u32[]{:S(2)}) collective-permute-start(bf16[768,1536]{0,1:T(8,128)(2,1)} %collective-permute-done), channel_id=1, source_target_pairs={{0,1},{1,2},{2,3},{3,0},{4,5},{5,6},{6,7},{7,4},{8,9},{9,10},{10,1... | collective-permute-start | bytes 7077896 | tf_op jit(solution)/shard_map/ppermute | solution.py:48
  46.2 57.3 %collective-permute-start.2 = (bf16[768,1536]{0,1:T(8,128)(2,1)}, bf16[768,1536]{0,1:T(8,128)(2,1)}, u32[]{:S(2)}, u32[]{:S(2)}) collective-permute-start(bf16[768,1536]{0,1:T(8,128)(2,1)} %bitcast.2), channel_id=1, source_target_pairs={{0,3},{1,0},{2,1},{3,2},{4,7},{5,4},{6,5},{7,6},{8,11},{9,8},{10,9... | collective-permute-start | bytes 7077896 | tf_op jit(solution)/shard_map/ppermute | solution.py:51
  123.2 778.8 %reduce-scatter.2.cloned.1.call-start = ((), (), s32[]{:S(2)}) async-start(), calls=%async_computation.1 | async-start | bytes 23592960 | tf_op jit(solution)/shard_map/reduce_scatter | solution.py:64
  765.0 136.9 %copy-start.3 = (f32[768,3]{0,1:T(4,128)S(1)}, f32[768,3]{0,1:T(4,128)}, u32[]{:S(2)}) copy-start(f32[768,3]{0,1:T(4,128)} %copy-done.2) | copy-start | bytes 27652
  765.1 284.0 %all-reduce.4.cloned.1.call-start = ((), (), s32[]{:S(2)}) async-start(), calls=%async_computation.2 | async-start | bytes 6291456 | tf_op jit(solution)/shard_map/psum | solution.py:71
  910.8 143.5 %copy-start.1 = (bf16[3,512,512]{2,1,0:T(8,128)(2,1)S(1)}, bf16[3,512,512]{2,1,0:T(8,128)(2,1)}, u32[]{:S(2)}) copy-start(bf16[3,512,512]{2,1,0:T(8,128)(2,1)} %param.7) | copy-start | bytes 4718596
Sparse Core Ops, SparseCore 0:
  123.3 571.2 all-reduce.5
  765.2 136.7 reduce-scatter.1
  910.9 138.1 all-reduce.3
